TPU v7x, 128 devices: a whole 4x4x4 slice. The times are simulated.
128 devices in a mesh: grp: 8 (over y, core), dev: 16 (over x, z).
Axes of the slice: x: 4, y: 4, z: 4, core: 2. Of those that a mesh axis runs over, the one named last changes fastest.
Arguments:
- suffix_queries: bfloat16 [16384, 2048], P(('grp', 'dev')), may hold values from -12 to 12
- suffix_keys: bfloat16 [16384, 2048], P(('grp', 'dev')), may hold values from -12 to 12
- suffix_values: bfloat16 [16384, 2048], P(('grp', 'dev')), may hold values from -6 to 6
- layer_input: bfloat16 [16384, 2048], P(('grp', 'dev')), may hold values from -6 to 6
- suffix_lengths: int32 [128, 8], P(('grp', 'dev')), may hold values from 1 to 32, as said below
- request_group: int32 [128, 8], P(('grp', 'dev')), may hold values from 0 to 7, as said below
- prefix_keys: bfloat16 [8, 4096, 2048], P('grp', None, 'dev'), may hold values from -12 to 12
- prefix_values: bfloat16 [8, 4096, 2048], P('grp', None, 'dev'), may hold values from -6 to 6
- up_weight: bfloat16 [2048, 8192], P(None, ('grp', 'dev')), may hold values from -0.125 to 0.125
- up_bias: bfloat16 [8192], P(('grp', 'dev')), may hold values from -3 to 3
- down_weight: bfloat16 [8192, 2048], P(('grp', 'dev')), may hold values from -0.0625 to 0.0625
- down_bias: float32 [2048], replicated, may hold values from -3 to 3
- attn_gain: float32 [2048], replicated, may hold values from 0.5 to 1.5
- attn_shift: float32 [2048], replicated, may hold values from -2 to 2
- out_gain: float32 [2048], replicated, may hold values from 0.5 to 1.5
- out_shift: float32 [2048], replicated, may hold values from -2 to 2
Outputs:
- layer_output: bfloat16 [16384, 2048], P(('grp', 'dev'))
Inputs may be any that keep to these rules, and one draw needn't show every extreme that they name: `suffix_lengths`: each row lists one device's 8 requests in slot order; they fill its 128 slots exactly, and at least one of them has 32 tokens. `request_group`: the 8 requests of one row name every prefix exactly once.
All inputs are finite; a program needn't handle non-finite values.
Results may differ from a plain program's by a relative error of at most 0.014.
Values may be sent and summed in bfloat16 or wider, within the bound.
A program may use at most 128 MiB of HBM per device.

v0:
```python
import math
import jax
import jax.numpy as jnp
from jax import lax
from jax.sharding import PartitionSpec as P

HD = 128
norm_eps = 1e-12


def layer_norm(summed, norm_gain, norm_shift):
    row_mean = jnp.mean(summed, axis=-1, keepdims=True)
    centred = summed - row_mean
    spread = jnp.mean(centred * centred, axis=-1, keepdims=True)
    return centred * lax.rsqrt(spread + norm_eps) * norm_gain + norm_shift


def request_layout(lengths, slot_count):
    end_points = jnp.cumsum(lengths)
    starts = end_points - lengths
    positions = lax.iota(jnp.int32, slot_count)
    member = (positions[:, None] >= starts[None, :]) & (positions[:, None] < end_points[None, :])
    slot_ids = lax.iota(jnp.int32, lengths.shape[0])
    segment = jnp.sum(jnp.where(member, slot_ids[None, :], 0), axis=1)
    return (starts, segment)


def expand_rows(piece_rows, up_matrix, up_offset):
    product = jnp.dot(piece_rows, up_matrix, preferred_element_type=jnp.float32)
    return jax.nn.gelu(product + up_offset.astype(jnp.float32), approximate=True).astype(
        jnp.bfloat16
    )


def attend_prefix(arrived, cache_keys, cache_values):
    sources, row_count, part_width = arrived.shape
    local_heads = part_width // HD
    per_block = math.gcd(sources, max(1, 512 // row_count))
    query_blocks = arrived.reshape(sources // per_block, per_block * row_count, local_heads, HD)
    key_heads = cache_keys.reshape(-1, local_heads, HD)
    value_heads = cache_values.reshape(-1, local_heads, HD)

    def one_block(query_block):
        scores = jnp.einsum(
            "qhd,khd->hqk", query_block, key_heads, preferred_element_type=jnp.float32
        ) * HD ** (-0.5)
        row_top = jnp.max(scores, axis=2).astype(jnp.bfloat16)
        weights = jnp.exp(
            scores - lax.optimization_barrier(row_top).astype(jnp.float32)[:, :, None]
        )
        row_sum = jnp.sum(weights, axis=2)
        mixed_sum = jnp.einsum(
            "hqk,khd->qhd",
            weights.astype(jnp.bfloat16),
            value_heads,
            preferred_element_type=jnp.float32,
        )
        answer = (mixed_sum / row_sum.T[:, :, None]).astype(jnp.bfloat16)
        return (answer.reshape(-1, part_width), row_top.T, row_sum.T.astype(jnp.bfloat16))

    answer, row_top, row_sum = lax.map(one_block, query_blocks)
    return (
        answer.reshape(sources, row_count, part_width),
        row_top.reshape(sources, row_count, local_heads),
        row_sum.reshape(sources, row_count, local_heads),
    )


def attend_suffix(query_rows, key_rows, value_rows, segment, head_count):
    slot_count = query_rows.shape[0]
    query_heads = query_rows.reshape(slot_count, head_count, HD)
    key_heads = key_rows.reshape(slot_count, head_count, HD)
    value_heads = value_rows.reshape(slot_count, head_count, HD)
    scores = jnp.einsum(
        "qhd,khd->hqk", query_heads, key_heads, preferred_element_type=jnp.float32
    ) * HD ** (-0.5)
    positions = lax.iota(jnp.int32, slot_count)
    visible = ((segment[:, None] == segment[None, :]) & (positions[None, :] <= positions[:, None]))[
        None
    ]
    row_top = jnp.max(jnp.where(visible, scores, -jnp.inf), axis=2)
    weights = jnp.where(visible, jnp.exp(scores - row_top[:, :, None]), 0.0)
    row_sum = jnp.sum(weights, axis=2)
    mixed_sum = jnp.einsum(
        "hqk,khd->qhd",
        weights.astype(jnp.bfloat16),
        value_heads,
        preferred_element_type=jnp.float32,
    )
    return (row_top.T, row_sum.T, mixed_sum)


def merge_parts(far_answer, far_top, far_sum, own_top, own_sum, own_mixed):
    far_top = far_top.astype(jnp.float32)
    far_sum = far_sum.astype(jnp.float32)
    joint_top = jnp.maximum(far_top, own_top)
    far_weight = jnp.exp(far_top - joint_top) * far_sum
    own_weight = jnp.exp(own_top - joint_top)
    numerator = (
        far_weight[:, :, None] * far_answer.astype(jnp.float32) + own_weight[:, :, None] * own_mixed
    )
    return numerator / (far_weight + own_weight * own_sum)[:, :, None]


def on_device(
    suffix_queries,
    suffix_keys,
    suffix_values,
    layer_input,
    suffix_lengths,
    request_group,
    prefix_keys,
    prefix_values,
    up_weight,
    up_bias,
    down_weight,
    down_bias,
    attn_gain,
    attn_shift,
    out_gain,
    out_shift,
):
    slot_count, model_width = suffix_queries.shape
    head_count = model_width // HD
    group_count = lax.axis_size("grp")
    column_count = lax.axis_size("dev")
    part_width = model_width // column_count
    local_heads = part_width // HD
    capacity = 2 * slot_count // group_count
    lengths = suffix_lengths[0]
    groups = request_group[0]
    request_total = lengths.shape[0]
    starts, segment = request_layout(lengths, slot_count)
    anchor = jnp.zeros((), jnp.int32)
    padded = jnp.concatenate(
        [suffix_queries, jnp.zeros((capacity, model_width), jnp.bfloat16)], axis=0
    )
    slot_rank = lax.iota(jnp.int32, capacity)
    outgoing = jnp.zeros((group_count, column_count, capacity, part_width), jnp.bfloat16)
    for request in range(request_total):
        taken = lax.dynamic_slice_in_dim(padded, starts[request], capacity, 0)
        taken = jnp.where((slot_rank < lengths[request])[:, None], taken, jnp.zeros_like(taken))
        split_rows = taken.reshape(capacity, column_count, part_width).transpose(1, 0, 2)
        outgoing = lax.dynamic_update_slice(
            outgoing, split_rows[None], (groups[request], anchor, anchor, anchor)
        )
    cache_keys = prefix_keys[0]
    cache_values = prefix_values[0]
    answer_part, top_part, sum_part = attend_prefix(
        lax.all_to_all(
            outgoing.reshape(group_count * column_count, capacity, part_width),
            ("grp", "dev"),
            split_axis=0,
            concat_axis=0,
            tiled=True,
        ),
        cache_keys,
        cache_values,
    )
    answer = lax.all_to_all(answer_part, ("grp", "dev"), split_axis=0, concat_axis=0, tiled=True)
    far_top = lax.all_to_all(top_part, ("grp", "dev"), split_axis=0, concat_axis=0, tiled=True)
    far_sum = lax.all_to_all(sum_part, ("grp", "dev"), split_axis=0, concat_axis=0, tiled=True)
    answer = answer.reshape(group_count, column_count, capacity, part_width)
    far_top = far_top.reshape(group_count, column_count, capacity, local_heads)
    far_sum = far_sum.reshape(group_count, column_count, capacity, local_heads)
    placed_answer = jnp.zeros((slot_count + capacity, model_width), jnp.bfloat16)
    placed_top = jnp.zeros((slot_count + capacity, head_count), jnp.bfloat16)
    placed_sum = jnp.zeros((slot_count + capacity, head_count), jnp.bfloat16)
    for request in range(request_total):
        own_answer = (
            lax.dynamic_index_in_dim(answer, groups[request], 0, keepdims=False)
            .transpose(1, 0, 2)
            .reshape(capacity, model_width)
        )
        own_top_rows = (
            lax.dynamic_index_in_dim(far_top, groups[request], 0, keepdims=False)
            .transpose(1, 0, 2)
            .reshape(capacity, head_count)
        )
        own_sum_rows = (
            lax.dynamic_index_in_dim(far_sum, groups[request], 0, keepdims=False)
            .transpose(1, 0, 2)
            .reshape(capacity, head_count)
        )
        placed_answer = lax.dynamic_update_slice(
            placed_answer, own_answer, (starts[request], anchor)
        )
        placed_top = lax.dynamic_update_slice(placed_top, own_top_rows, (starts[request], anchor))
        placed_sum = lax.dynamic_update_slice(placed_sum, own_sum_rows, (starts[request], anchor))
    own_top, own_sum, own_mixed = attend_suffix(
        suffix_queries, suffix_keys, suffix_values, segment, head_count
    )
    far_rows = placed_answer[:slot_count].reshape(slot_count, head_count, HD)
    context = merge_parts(
        far_rows, placed_top[:slot_count], placed_sum[:slot_count], own_top, own_sum, own_mixed
    )
    hidden_state = layer_norm(
        layer_input.astype(jnp.float32) + context.reshape(slot_count, model_width),
        attn_gain,
        attn_shift,
    ).astype(jnp.bfloat16)
    up_slice, bias_slice, down_slice = (
        lax.all_gather(up_weight, "grp", axis=1, tiled=True),
        lax.all_gather(up_bias, "grp", axis=0, tiled=True),
        lax.all_gather(down_weight, "grp", axis=0, tiled=True),
    )
    activation = expand_rows(
        lax.all_gather(hidden_state, "dev", axis=0, tiled=True), up_slice, bias_slice
    )
    mlp_sum = lax.psum_scatter(
        jnp.dot(activation, down_slice, preferred_element_type=jnp.float32).astype(jnp.bfloat16),
        "dev",
        scatter_dimension=0,
        tiled=True,
    ).astype(jnp.float32)
    return layer_norm(
        hidden_state.astype(jnp.float32) + mlp_sum + down_bias, out_gain, out_shift
    ).astype(jnp.bfloat16)


def solution(mesh):
    placed = (
        P(("grp", "dev"), None),
        P(("grp", "dev"), None),
        P(("grp", "dev"), None),
        P(("grp", "dev"), None),
        P(("grp", "dev"), None),
        P(("grp", "dev"), None),
        P("grp", None, "dev"),
        P("grp", None, "dev"),
        P(None, ("grp", "dev")),
        P(("grp", "dev")),
        P(("grp", "dev"), None),
        P(),
        P(),
        P(),
        P(),
        P(),
    )
    return jax.shard_map(
        on_device, mesh=mesh, in_specs=placed, out_specs=P(("grp", "dev"), None), check_vma=False
    )
```

profile of v0, /device:TPU:0, one launch (start us, length us, event | category | flops | bytes accessed | tf_op | source)
XLA Modules:
  0.0 412.4 jit_solution(14731411691771604662)
XLA Ops:
  57.2 11.2 %all-to-all-start = ((bf16[128,32,128]{2,1,0:T(8,128)(2,1)}), bf16[128,32,128]{2,1,0:T(8,128)(2,1)S(1)}, u32[]{:S(2)}, u32[]{:S(2)}) async-start(bf16[128,32,128]{2,1,0:T(8,128)(2,1)} %bitcast.51), calls=%async_computation | async-start | bytes 2097152 | tf_op jit(solution)/shard_map/all_to_all | solution.py:150
  69.2 18.3 %all-to-all-done = bf16[128,32,128]{2,1,0:T(8,128)(2,1)S(1)} async-done(((bf16[128,32,128]{2,1,0:T(8,128)(2,1)}), bf16[128,32,128]{2,1,0:T(8,128)(2,1)S(1)}, u32[]{:S(2)}, u32[]{:S(2)}) %all-to-all-start) | async-done | bytes 1048608 | tf_op jit(solution)/shard_map/all_to_all | solution.py:150
  87.5 41.1 %while.14 = (s32[]{:T(128)}, bf16[8,512,128]{2,1,0:T(8,128)(2,1)}, bf16[8,512,1]{1,0,2:T(8,128)(2,1)S(1)}, bf16[8,512,1]{1,0,2:T(8,128)(2,1)S(1)}, bf16[8,512,1,...) while((s32[]{:T(128)}, bf16[8,512,128]{2,1,0:T(8,128)(2,1)}, ...), condition=%wide.region_4.5_spmd, body=%wide.region_1.4_spmd.sunk | while | flops 1090650112 | bytes 31745168 | solution.py:61
  126.3 2.2 fusion.119
  129.3 4.6 %all-to-all-start.2 = ((bf16[128,32,1]{1,2,0:T(2,128)(2,1)}), bf16[128,32,1]{1,2,0:T(2,128)(2,1)S(1)}, u32[]{:S(2)}, u32[]{:S(2)}) async-start(bf16[128,32,1]{1,2,0:T(2,128)(2,1)} %reshape.401), calls=%async_computation.2 | async-start | bytes 131072 | tf_op jit(solution)/shard_map/all_to_all | solution.py:162
  134.6 8.8 %all-to-all-done.2 = bf16[128,32,1]{1,2,0:T(2,128)(2,1)S(1)} async-done(((bf16[128,32,1]{1,2,0:T(2,128)(2,1)}), bf16[128,32,1]{1,2,0:T(2,128)(2,1)S(1)}, u32[]{:S(2)}, u32[]{:S(2)}) %all-to-all-start.2) | async-done | bytes 8224 | tf_op jit(solution)/shard_map/all_to_all | solution.py:162
  143.4 4.6 %all-to-all-start.1 = ((bf16[128,32,1]{1,2,0:T(2,128)(2,1)}), bf16[128,32,1]{1,2,0:T(2,128)(2,1)S(1)}, u32[]{:S(2)}, u32[]{:S(2)}) async-start(bf16[128,32,1]{1,2,0:T(2,128)(2,1)} %reshape.400), calls=%async_computation.1 | async-start | bytes 131072 | tf_op jit(solution)/shard_map/all_to_all | solution.py:161
  148.0 9.4 %all-to-all-done.1 = bf16[128,32,1]{1,2,0:T(2,128)(2,1)S(1)} async-done(((bf16[128,32,1]{1,2,0:T(2,128)(2,1)}), bf16[128,32,1]{1,2,0:T(2,128)(2,1)S(1)}, u32[]{:S(2)}, u32[]{:S(2)}) %all-to-all-start.1) | async-done | bytes 8224 | tf_op jit(solution)/shard_map/all_to_all | solution.py:161
  157.4 4.6 %all-to-all-start.3 = ((bf16[128,32,128]{2,1,0:T(8,128)(2,1)}), bf16[128,32,128]{2,1,0:T(8,128)(2,1)S(1)}, u32[]{:S(2)}, u32[]{:S(2)}) async-start(bf16[128,32,128]{2,1,0:T(8,128)(2,1)} %bitcast.380), calls=%async_computation.3 | async-start | bytes 2097152 | tf_op jit(solution)/shard_map/all_to_all | solution.py:160
  170.3 10.7 %all-to-all-done.3 = bf16[128,32,128]{2,1,0:T(8,128)(2,1)S(1)} async-done(((bf16[128,32,128]{2,1,0:T(8,128)(2,1)}), bf16[128,32,128]{2,1,0:T(8,128)(2,1)S(1)}, u32[]{:S(2)}, u32[]{:S(2)}) %all-to-all-start.3) | async-done | bytes 1048608 | tf_op jit(solution)/shard_map/all_to_all | solution.py:160
  187.3 4.9 %dynamic_update_slice.131 = bf16[160,2048]{0,1:T(8,128)(2,1)S(1)} dynamic-update-slice(bf16[160,2048]{0,1:T(8,128)(2,1)S(1)} %broadcast_in_dim.168, bf16[32,2048]{0,1:T(8,128)(2,1)} %bitcast.379, s32[]{:T(128)S(6)} %select_n.134, s32[]{:T(128)} %constant.96.clone.1) | dynamic-update-slice | bytes 262148 | tf_op jit(solution)/shard_map/dynamic_update_slice | solution.py:185
  192.2 5.9 %dynamic_update_slice.132 = bf16[160,2048]{0,1:T(8,128)(2,1)S(1)} dynamic-update-slice(bf16[160,2048]{0,1:T(8,128)(2,1)S(1)} %dynamic_update_slice.131, bf16[32,2048]{0,1:T(8,128)(2,1)} %bitcast.378, s32[]{:T(128)S(6)} %select_n.137, s32[]{:T(128)} %constant.96.clone.1) | dynamic-update-slice | bytes 262148 | tf_op jit(solution)/shard_map/dynamic_update_slice | solution.py:185
  198.1 5.9 %dynamic_update_slice.133 = bf16[160,2048]{0,1:T(8,128)(2,1)S(1)} dynamic-update-slice(bf16[160,2048]{0,1:T(8,128)(2,1)S(1)} %dynamic_update_slice.132, bf16[32,2048]{0,1:T(8,128)(2,1)} %bitcast.377, s32[]{:T(128)S(6)} %select_n.140, s32[]{:T(128)} %constant.96.clone.1) | dynamic-update-slice | bytes 262148 | tf_op jit(solution)/shard_map/dynamic_update_slice | solution.py:185
  204.1 5.9 %dynamic_update_slice.134 = bf16[160,2048]{0,1:T(8,128)(2,1)S(1)} dynamic-update-slice(bf16[160,2048]{0,1:T(8,128)(2,1)S(1)} %dynamic_update_slice.133, bf16[32,2048]{0,1:T(8,128)(2,1)} %bitcast.376, s32[]{:T(128)S(6)} %select_n.143, s32[]{:T(128)} %constant.96.clone.1) | dynamic-update-slice | bytes 262148 | tf_op jit(solution)/shard_map/dynamic_update_slice | solution.py:185
  210.0 5.9 %dynamic_update_slice.135 = bf16[160,2048]{0,1:T(8,128)(2,1)S(1)} dynamic-update-slice(bf16[160,2048]{0,1:T(8,128)(2,1)S(1)} %dynamic_update_slice.134, bf16[32,2048]{0,1:T(8,128)(2,1)} %bitcast.375, s32[]{:T(128)S(6)} %select_n.146, s32[]{:T(128)} %constant.96.clone.1) | dynamic-update-slice | bytes 262148 | tf_op jit(solution)/shard_map/dynamic_update_slice | solution.py:185
  216.0 4.0 dynamic_update_slice.136
  220.0 4.0 dynamic_update_slice.137
  224.0 4.2 %dynamic_update_slice.138 = bf16[160,2048]{0,1:T(8,128)(2,1)S(1)} dynamic-update-slice(bf16[160,2048]{0,1:T(8,128)(2,1)S(1)} %dynamic_update_slice.137, bf16[32,2048]{0,1:T(8,128)(2,1)S(1)} %bitcast.372, s32[]{:T(128)S(6)} %select_n.155, s32[]{:T(128)} %constant.96.clone.1) | dynamic-update-slice | bytes 262148 | tf_op jit(solution)/shard_map/dynamic_update_slice | solution.py:185
  228.3 2.8 fusion.36
  235.9 12.8 %all-reduce.1 = bf16[512]{0:T(512)(128)(2,1)S(1)} all-reduce(bf16[512]{0:T(512)(128)(2,1)S(1)} %dynamic-update-slice), channel_id=1, replica_groups=mesh['grp'=8,'dev'=16] {'grp'}, use_global_device_ids=true, to_apply=%add.1 | all-reduce | flops 512 | bytes 2048
  248.8 52.0 %all-gather.4.cloned.1.call-done = bf16[2048,2048]{1,0:T(8,128)(2,1)} async-done(((bf16[128,2048]{1,0:T(8,128)(2,1)}), bf16[2048,2048]{1,0:T(8,128)(2,1)}) %all-gather.4.cloned.1.call-update) | async-done | bytes 8388624 | tf_op jit(solution)/shard_map/all_gather | solution.py:208
  300.8 15.2 %convolution_convert_fusion = bf16[2048,2048]{1,0:T(8,128)(2,1)} fusion(bf16[512,2048]{1,0:T(8,128)(2,1)} %all-gather.8.cloned.1.call-done, bf16[2048,2048]{1,0:T(8,128)(2,1)} %all-gather.4.cloned.1.call-done, bf16[2048,512]{0,1:T(8,128)(2,1)} %all-gather.6.cloned.1.call-done, f32[512]{0:T(512)S(1)} %convert_element_type.97), kind=kOutput, calls=%fused_computation.17 | convolution fusion | flops 8604614656 | bytes 20973568 | tf_op jit(solution)/shard_map/dot_general | solution.py:211
  316.1 84.9 %reduce-scatter.2.cloned.1.call-done = bf16[128,2048]{1,0:T(8,128)(2,1)} async-done(((bf16[2048,2048]{1,0:T(8,128)(2,1)}), bf16[128,2048]{1,0:T(8,128)(2,1)}) %reduce-scatter.2.cloned.1.call-update) | async-done | bytes 524304 | tf_op jit(solution)/shard_map/reduce_scatter | solution.py:210
  403.7 2.2 add_convert_fusion
  (215 shorter events, 82.7 us)
Async XLA Ops:
  6.5 157.7 %copy-start = (bf16[128,2048]{1,0:T(8,128)(2,1)S(1)}, bf16[128,2048]{1,0:T(8,128)(2,1)}, u32[]{:S(2)}) copy-start(bf16[128,2048]{1,0:T(8,128)(2,1)} %param.19) | copy-start | bytes 1572868
  6.5 80.9 %copy-start.1 = (bf16[1,4096,128]{2,1,0:T(8,128)(2,1)S(1)}, bf16[1,4096,128]{2,1,0:T(8,128)(2,1)}, u32[]{:S(2)}) copy-start(bf16[1,4096,128]{2,1,0:T(8,128)(2,1)} %param.24) | copy-start | bytes 3145732
  6.5 242.2 %all-gather.6.cloned.1.call-start = ((), (), s32[]{:S(2)}) async-start(), calls=%async_computation.6 | async-start | bytes 2359296 | tf_op jit(solution)/shard_map/all_gather | solution.py:203
  57.2 30.3 %all-to-all-start = ((bf16[128,32,128]{2,1,0:T(8,128)(2,1)}), bf16[128,32,128]{2,1,0:T(8,128)(2,1)S(1)}, u32[]{:S(2)}, u32[]{:S(2)}) async-start(bf16[128,32,128]{2,1,0:T(8,128)(2,1)} %bitcast.51), calls=%async_computation | async-start | bytes 2097152 | tf_op jit(solution)/shard_map/all_to_all | solution.py:150
  68.4 180.4 %all-gather.8.cloned.1.call-start = ((), (), s32[]{:S(2)}) async-start(), calls=%async_computation.7 | async-start | bytes 2359296 | tf_op jit(solution)/shard_map/all_gather | solution.py:205
  87.5 60.5 %copy-start.7 = (s32[1,8]{1,0:T(1,128)S(1)}, s32[1,8]{1,0:T(1,128)}, u32[]{:S(2)}) copy-start(s32[1,8]{1,0:T(1,128)} %param.22) | copy-start | bytes 100
  87.5 76.8 %copy-start.4 = (bf16[128,2048]{1,0:T(8,128)(2,1)S(1)}, bf16[128,2048]{1,0:T(8,128)(2,1)}, u32[]{:S(2)}) copy-start(bf16[128,2048]{1,0:T(8,128)(2,1)} %param.18) | copy-start | bytes 1572868
  94.0 1.5 copy-start.12
  99.1 1.5 copy-start.12
  104.3 1.5 copy-start.12
  129.3 14.0 %all-to-all-start.2 = ((bf16[128,32,1]{1,2,0:T(2,128)(2,1)}), bf16[128,32,1]{1,2,0:T(2,128)(2,1)S(1)}, u32[]{:S(2)}, u32[]{:S(2)}) async-start(bf16[128,32,1]{1,2,0:T(2,128)(2,1)} %reshape.401), calls=%async_computation.2 | async-start | bytes 131072 | tf_op jit(solution)/shard_map/all_to_all | solution.py:162
  143.4 14.0 %all-to-all-start.1 = ((bf16[128,32,1]{1,2,0:T(2,128)(2,1)}), bf16[128,32,1]{1,2,0:T(2,128)(2,1)S(1)}, u32[]{:S(2)}, u32[]{:S(2)}) async-start(bf16[128,32,1]{1,2,0:T(2,128)(2,1)} %reshape.400), calls=%async_computation.1 | async-start | bytes 131072 | tf_op jit(solution)/shard_map/all_to_all | solution.py:161
  157.4 23.7 %all-to-all-start.3 = ((bf16[128,32,128]{2,1,0:T(8,128)(2,1)}), bf16[128,32,128]{2,1,0:T(8,128)(2,1)S(1)}, u32[]{:S(2)}, u32[]{:S(2)}) async-start(bf16[128,32,128]{2,1,0:T(8,128)(2,1)} %bitcast.380), calls=%async_computation.3 | async-start | bytes 2097152 | tf_op jit(solution)/shard_map/all_to_all | solution.py:160
  162.0 138.8 %all-gather.4.cloned.1.call-start = ((), (), s32[]{:S(2)}) async-start(), calls=%async_computation.5 | async-start | bytes 8912896 | tf_op jit(solution)/shard_map/all_gather | solution.py:208
  228.3 4.4 %copy-start.3 = (bf16[128,2048]{1,0:T(8,128)(2,1)S(1)}, bf16[128,2048]{1,0:T(8,128)(2,1)}, u32[]{:S(2)}) copy-start(bf16[128,2048]{1,0:T(8,128)(2,1)} %param.21) | copy-start | bytes 1572868
  228.3 4.9 %copy-start.8 = (f32[2048]{0:T(1024)S(1)}, f32[2048]{0:T(1024)}, u32[]{:S(2)}) copy-start(f32[2048]{0:T(1024)} %param.31) | copy-start | bytes 24580
  228.3 4.9 %copy-start.9 = (f32[2048]{0:T(1024)S(1)}, f32[2048]{0:T(1024)}, u32[]{:S(2)}) copy-start(f32[2048]{0:T(1024)} %param.30) | copy-start | bytes 24580
  231.1 3.3 copy-start.14
  231.1 4.5 %copy-start.13 = (bf16[64]{0:T(256)(128)(2,1)S(1)}, bf16[64]{0:T(256)(128)(2,1)}, u32[]{:S(2)}) copy-start(bf16[64]{0:T(256)(128)(2,1)} %param.27) | copy-start | bytes 388
  234.3 166.6 %reduce-scatter.2.cloned.1.call-start = ((), (), s32[]{:S(2)}) async-start(), calls=%async_computation.8 | async-start | bytes 8912896 | tf_op jit(solution)/shard_map/reduce_scatter | solution.py:210
  316.0 84.9 %copy-start.2 = (bf16[128,2048]{1,0:T(8,128)(2,1)S(1)}, bf16[128,2048]{1,0:T(8,128)(2,1)}, u32[]{:S(2)}) copy-start(bf16[128,2048]{1,0:T(8,128)(2,1)} %add_convert_fusion.1) | copy-start | bytes 1572868
  316.0 84.9 %copy-start.6 = (f32[2048]{0:T(1024)S(1)}, f32[2048]{0:T(1024)}, u32[]{:S(2)}) copy-start(f32[2048]{0:T(1024)} %param.29) | copy-start | bytes 24580
  316.0 87.6 %copy-start.10 = (f32[2048]{0:T(1024)S(1)}, f32[2048]{0:T(1024)}, u32[]{:S(2)}) copy-start(f32[2048]{0:T(1024)} %param.33) | copy-start | bytes 24580
  316.0 87.6 %copy-start.11 = (f32[2048]{0:T(1024)S(1)}, f32[2048]{0:T(1024)}, u32[]{:S(2)}) copy-start(f32[2048]{0:T(1024)} %param.32) | copy-start | bytes 24580
  (6 other events, 8.6 us)
Sparse Core Ops, SparseCore 0:
  9.1 27.6 all-gather.5
  71.0 26.2 all-gather.7
  234.5 66.3 all-gather.3
  316.2 84.7 reduce-scatter.1
where the time goes:
time: 414 us; the launch traced here: 412 us
  waiting for transfers between devices  186 us (45%)
  local copies, waits for them, and re-layouts  69.7 us (17%)
  matrix products  46.3 us (11%)
  between operations  44.2 us (11%)
  other arithmetic  28.4 us (7%)
  starting transfers between devices  25.1 us (6%)
  blocking collectives  12.8 us (3%)
    reduce_scatter x1, waiting for transfers between devices, on_device(): lax.psum_scatter(jnp.dot(activation, down_slice, preferred_element_type=j...  84.9 us
    all_gather x1, waiting for transfers between devices, on_device(): lax.all_gather(hidden_state, 'dev', axis=0, tiled=True)  52 us
    dynamic_update_slice x8, local copies, waits for them, and re-layouts, on_device(): lax.dynamic_update_slice(placed_answer, own_answer, (starts[request], anc...  40.9 us
    all_to_all x1, waiting for transfers between devices, on_device(): lax.all_to_all(outgoing.reshape(group_count * column_count, capacity, par...  18.3 us
    dot_general x8, matrix products, one_block(): jnp.einsum('hqk,khd->qhd', weights.astype(jnp.bfloat16), value_heads, pre...  17.2 us
    dot_general x1, matrix products, on_device(): jnp.dot(activation, down_slice, preferred_element_type=jnp.float32)  15.2 us
    unnamed x1, blocking collectives  12.8 us
    reduce_sum x8, other arithmetic, one_block(): row_sum = jnp.sum(weights, axis=2)  12 us
  transfers between devices with their start and end apart: 8, of which 6 were waited for; matrix products, arithmetic and copies ran while one was open for 30% of the time, Pallas kernels for 0%

commit v1 on v0

--- a/solution.py
+++ b/solution.py
@@ -3,9 +3,44 @@
 import jax.numpy as jnp
 from jax import lax
 from jax.sharding import PartitionSpec as P
+from jax.lax import axis_index, axis_size, ppermute
 
 HD = 128
 norm_eps = 1e-12
+
+
+def slot_change(message, dimension_no):
+    message = jnp.moveaxis(message, 0, dimension_no)
+    u1 = message.shape
+    y = message.reshape(
+        *u1[:dimension_no], u1[dimension_no] * u1[dimension_no + 1], *u1[dimension_no + 2 :]
+    )
+    return y
+
+
+def start_rounds(incoming_x, across, axis_k):
+    q_n = axis_size(across)
+    ix = 0
+    buffers = []
+    while ix < q_n:
+        buffers.append((ix, (ix + 1) % q_n))
+        ix = ix + 1
+    stack_in = []
+    for nth, dd in buffers:
+        stack_in.append((dd, nth))
+    known, small = ([], [])
+    p = 0
+    while p < q_n - 1:
+        if p % 2 == 0:
+            known.append(ppermute(known[-1] if known else incoming_x, across, buffers))
+        else:
+            small.append(ppermute(small[-1] if small else incoming_x, across, stack_in))
+        p += 1
+    tall = jnp.stack([*known[::-1], incoming_x, *small], axis=0)
+    earlier = axis_index(across) - len(known)
+    tall = tall[(jnp.arange(q_n) - earlier) % q_n]
+    y_new = slot_change(tall, axis_k)
+    return y_new
 
 
 def layer_norm(summed, norm_gain, norm_shift):
@@ -204,9 +239,7 @@
         lax.all_gather(up_bias, "grp", axis=0, tiled=True),
         lax.all_gather(down_weight, "grp", axis=0, tiled=True),
     )
-    activation = expand_rows(
-        lax.all_gather(hidden_state, "dev", axis=0, tiled=True), up_slice, bias_slice
-    )
+    activation = expand_rows(start_rounds(hidden_state, "dev", 0), up_slice, bias_slice)
     mlp_sum = lax.psum_scatter(
         jnp.dot(activation, down_slice, preferred_element_type=jnp.float32).astype(jnp.bfloat16),
         "dev",

time: 414 us -> 501 us (1.21); the launches traced: 412 us -> 492 us
  starting transfers between devices: 25.1 us -> 64.2 us
  local copies, waits for them, and re-layouts: 69.7 us -> 95.3 us
  matrix products: 46.3 us -> 55.8 us
    ppermute x0 -> x15, waiting for transfers between devices: none -> 63.8 us  [the longest x8 62.3 us: start_rounds(): known.append(ppermute(known[-1] if known else incoming_x, across, buffers))]
    all_gather x1 -> x0, waiting for transfers between devices: 52 us -> none  [on_device(): lax.all_gather(hidden_state, 'dev', axis=0, tiled=True)]
    ppermute x0 -> x15, starting transfers between devices: none -> 39.1 us  [the longest x7 38.1 us: start_rounds(): small.append(ppermute(small[-1] if small else incoming_x, across, stack_in))]
    unnamed x33 -> x62, local copies, waits for them, and re-layouts: 1.93 us -> 23.7 us
    dot_general x8, matrix products: 10.7 us -> 21.2 us  [one_block(): jnp.einsum('qhd,khd->hqk', query_block, key_heads, preferred_element_type...]
    gather x0 -> x1, local copies, waits for them, and re-layouts: none -> 8.37 us  [start_rounds(): tall = tall[(jnp.arange(q_n) - earlier) % q_n]]
    reduce_scatter x1, waiting for transfers between devices: 84.9 us -> 78.8 us  [on_device(): lax.psum_scatter(jnp.dot(activation, down_slice, preferred_element_type=j...]
  transfers between devices with their start and end apart: 8 -> 22, of which waited for: 6 -> 14; matrix products, arithmetic and copies ran while one was open for 30% -> 8% of each run, Pallas kernels for 0% -> 0%
where the time goes in v1:
time: 501 us; the launch traced here: 492 us
  waiting for transfers between devices  191 us (38%)
  local copies, waits for them, and re-layouts  95.3 us (19%)
  starting transfers between devices  64.2 us (13%)
  matrix products  55.8 us (11%)
  between operations  44.4 us (9%)
  other arithmetic  27.5 us (5%)
  blocking collectives  12.8 us (3%)
    reduce_scatter x1, waiting for transfers between devices, on_device(): lax.psum_scatter(jnp.dot(activation, down_slice, preferred_element_type=j...  78.8 us
    ppermute x8, waiting for transfers between devices, start_rounds(): known.append(ppermute(known[-1] if known else incoming_x, across, buffers))  62.3 us
    dynamic_update_slice x8, local copies, waits for them, and re-layouts, on_device(): lax.dynamic_update_slice(placed_answer, own_answer, (starts[request], anc...  38.7 us
    ppermute x7, starting transfers between devices, start_rounds(): small.append(ppermute(small[-1] if small else incoming_x, across, stack_in))  38.1 us
    unnamed x62, local copies, waits for them, and re-layouts  23.7 us
    dot_general x8, matrix products, one_block(): jnp.einsum('qhd,khd->hqk', query_block, key_heads, preferred_element_type...  21.2 us
    all_to_all x1, waiting for transfers between devices, on_device(): lax.all_to_all(outgoing.reshape(group_count * column_count, capacity, par...  19 us
    dot_general x8, matrix products, one_block(): jnp.einsum('hqk,khd->qhd', weights.astype(jnp.bfloat16), value_heads, pre...  17.1 us
  transfers between devices with their start and end apart: 22, of which 14 were waited for; matrix products, arithmetic and copies ran while one was open for 8% of the time, Pallas kernels for 0%

profile of v1, /device:TPU:0, one launch (start us, length us, event | category | flops | bytes accessed | tf_op | source)
XLA Modules:
  0.0 492.0 jit_solution(6635212174220183825)
XLA Ops:
  56.2 11.2 %all-to-all-start = ((bf16[128,32,128]{2,1,0:T(8,128)(2,1)}), bf16[128,32,128]{2,1,0:T(8,128)(2,1)S(1)}, u32[]{:S(2)}, u32[]{:S(2)}) async-start(bf16[128,32,128]{2,1,0:T(8,128)(2,1)} %bitcast.51), calls=%async_computation | async-start | bytes 2097152 | tf_op jit(solution)/shard_map/all_to_all | solution.py:185
  67.5 19.0 %all-to-all-done = bf16[128,32,128]{2,1,0:T(8,128)(2,1)S(1)} async-done(((bf16[128,32,128]{2,1,0:T(8,128)(2,1)}), bf16[128,32,128]{2,1,0:T(8,128)(2,1)S(1)}, u32[]{:S(2)}, u32[]{:S(2)}) %all-to-all-start) | async-done | bytes 1048608 | tf_op jit(solution)/shard_map/all_to_all | solution.py:185
  86.5 51.6 %while.14 = (s32[]{:T(128)}, bf16[8,512,128]{2,1,0:T(8,128)(2,1)}, bf16[8,512,1]{1,0,2:T(8,128)(2,1)S(1)}, bf16[8,512,1]{1,0,2:T(8,128)(2,1)S(1)}, bf16[8,512,1,...) while((s32[]{:T(128)}, bf16[8,512,128]{2,1,0:T(8,128)(2,1)}, ...), condition=%wide.region_4.5_spmd, body=%wide.region_1.4_spmd.sunk | while | flops 1090650112 | bytes 31745668 | solution.py:96
  144.2 8.7 %all-to-all-done.1 = bf16[128,32,1]{1,2,0:T(2,128)(2,1)S(1)} async-done(((bf16[128,32,1]{1,2,0:T(2,128)(2,1)}), bf16[128,32,1]{1,2,0:T(2,128)(2,1)S(1)}, u32[]{:S(2)}, u32[]{:S(2)}) %all-to-all-start.1) | async-done | bytes 8224 | tf_op jit(solution)/shard_map/all_to_all | solution.py:196
  157.5 9.5 %all-to-all-done.2 = bf16[128,32,1]{1,2,0:T(2,128)(2,1)S(1)} async-done(((bf16[128,32,1]{1,2,0:T(2,128)(2,1)}), bf16[128,32,1]{1,2,0:T(2,128)(2,1)S(1)}, u32[]{:S(2)}, u32[]{:S(2)}) %all-to-all-start.2) | async-done | bytes 8224 | tf_op jit(solution)/shard_map/all_to_all | solution.py:197
  179.0 11.7 %all-to-all-done.3 = bf16[128,32,128]{2,1,0:T(8,128)(2,1)S(1)} async-done(((bf16[128,32,128]{2,1,0:T(8,128)(2,1)}), bf16[128,32,128]{2,1,0:T(8,128)(2,1)S(1)}, u32[]{:S(2)}, u32[]{:S(2)}) %all-to-all-start.3) | async-done | bytes 1048608 | tf_op jit(solution)/shard_map/all_to_all | solution.py:195
  198.5 6.0 %dynamic_update_slice.132 = bf16[160,2048]{0,1:T(8,128)(2,1)S(1)} dynamic-update-slice(bf16[160,2048]{0,1:T(8,128)(2,1)S(1)} %dynamic_update_slice.131, bf16[32,2048]{0,1:T(8,128)(2,1)} %bitcast.414, s32[]{:T(128)S(6)} %select_n.161, s32[]{:T(128)} %constant.114.clone.1) | dynamic-update-slice | bytes 262148 | tf_op jit(solution)/shard_map/dynamic_update_slice | solution.py:220
  204.4 5.9 %dynamic_update_slice.133 = bf16[160,2048]{0,1:T(8,128)(2,1)S(1)} dynamic-update-slice(bf16[160,2048]{0,1:T(8,128)(2,1)S(1)} %dynamic_update_slice.132, bf16[32,2048]{0,1:T(8,128)(2,1)} %bitcast.413, s32[]{:T(128)S(6)} %select_n.164, s32[]{:T(128)} %constant.114.clone.1) | dynamic-update-slice | bytes 262148 | tf_op jit(solution)/shard_map/dynamic_update_slice | solution.py:220
  210.4 5.9 %dynamic_update_slice.134 = bf16[160,2048]{0,1:T(8,128)(2,1)S(1)} dynamic-update-slice(bf16[160,2048]{0,1:T(8,128)(2,1)S(1)} %dynamic_update_slice.133, bf16[32,2048]{0,1:T(8,128)(2,1)} %bitcast.412, s32[]{:T(128)S(6)} %select_n.167, s32[]{:T(128)} %constant.114.clone.1) | dynamic-update-slice | bytes 262148 | tf_op jit(solution)/shard_map/dynamic_update_slice | solution.py:220
  216.4 5.9 %dynamic_update_slice.135 = bf16[160,2048]{0,1:T(8,128)(2,1)S(1)} dynamic-update-slice(bf16[160,2048]{0,1:T(8,128)(2,1)S(1)} %dynamic_update_slice.134, bf16[32,2048]{0,1:T(8,128)(2,1)} %bitcast.411, s32[]{:T(128)S(6)} %select_n.170, s32[]{:T(128)} %constant.114.clone.1) | dynamic-update-slice | bytes 262148 | tf_op jit(solution)/shard_map/dynamic_update_slice | solution.py:220
  238.9 15.2 %collective-permute-done = bf16[128,2048]{1,0:T(8,128)(2,1)S(1)} collective-permute-done((bf16[128,2048]{1,0:T(8,128)(2,1)S(1)}, bf16[128,2048]{1,0:T(8,128)(2,1)S(1)}, u32[]{:S(2)}, u32[]{:S(2)}) %collective-permute-start) | collective-permute-done | bytes 524320 | tf_op jit(solution)/shard_map/ppermute | solution.py:35
  259.4 9.9 %collective-permute-done.1 = bf16[128,2048]{1,0:T(8,128)(2,1)S(1)} collective-permute-done((bf16[128,2048]{1,0:T(8,128)(2,1)S(1)}, bf16[128,2048]{1,0:T(8,128)(2,1)S(1)}, u32[]{:S(2)}, u32[]{:S(2)}) %collective-permute-start.1) | collective-permute-done | bytes 524320 | tf_op jit(solution)/shard_map/ppermute | solution.py:35
  274.7 9.0 %collective-permute-done.2 = bf16[128,2048]{1,0:T(8,128)(2,1)S(1)} collective-permute-done((bf16[128,2048]{1,0:T(8,128)(2,1)S(1)}, bf16[128,2048]{1,0:T(8,128)(2,1)S(1)}, u32[]{:S(2)}, u32[]{:S(2)}) %collective-permute-start.2) | collective-permute-done | bytes 524320 | tf_op jit(solution)/shard_map/ppermute | solution.py:35
  283.6 5.3 %collective-permute-start.10 = (bf16[128,2048]{1,0:T(8,128)(2,1)S(1)}, bf16[128,2048]{1,0:T(8,128)(2,1)S(1)}, u32[]{:S(2)}, u32[]{:S(2)}) collective-permute-start(bf16[128,2048]{1,0:T(8,128)(2,1)S(1)} %collective-permute-done.9), channel_id=1, source_target_pairs={{1,0},{2,1},{3,2},{4,3},{5,4},{6,5},{7,6},{8,7},{9,8},{10,9},{11,1... | collective-permute-start | bytes 1572872 | tf_op jit(solution)/shard_map/ppermute | solution.py:37
  289.0 8.1 %collective-permute-done.3 = bf16[128,2048]{1,0:T(8,128)(2,1)S(1)} collective-permute-done((bf16[128,2048]{1,0:T(8,128)(2,1)S(1)}, bf16[128,2048]{1,0:T(8,128)(2,1)S(1)}, u32[]{:S(2)}, u32[]{:S(2)}) %collective-permute-start.3) | collective-permute-done | bytes 524320 | tf_op jit(solution)/shard_map/ppermute | solution.py:35
  303.2 6.4 %collective-permute-done.4 = bf16[128,2048]{1,0:T(8,128)(2,1)S(1)} collective-permute-done((bf16[128,2048]{1,0:T(8,128)(2,1)S(1)}, bf16[128,2048]{1,0:T(8,128)(2,1)S(1)}, u32[]{:S(2)}, u32[]{:S(2)}) %collective-permute-start.4) | collective-permute-done | bytes 524320 | tf_op jit(solution)/shard_map/ppermute | solution.py:35
  310.7 5.8 %collective-permute-start.12 = (bf16[128,2048]{1,0:T(8,128)(2,1)S(1)}, bf16[128,2048]{1,0:T(8,128)(2,1)}, u32[]{:S(2)}, u32[]{:S(2)}) collective-permute-start(bf16[128,2048]{1,0:T(8,128)(2,1)S(1)} %collective-permute-done.11), channel_id=1, source_target_pairs={{1,0},{2,1},{3,2},{4,3},{5,4},{6,5},{7,6},{8,7},{9,8},{10,9},{11,1... | collective-permute-start | bytes 1572872 | tf_op jit(solution)/shard_map/ppermute | solution.py:37
  316.5 6.5 %collective-permute-done.5 = bf16[128,2048]{1,0:T(8,128)(2,1)S(1)} collective-permute-done((bf16[128,2048]{1,0:T(8,128)(2,1)S(1)}, bf16[128,2048]{1,0:T(8,128)(2,1)S(1)}, u32[]{:S(2)}, u32[]{:S(2)}) %collective-permute-start.5) | collective-permute-done | bytes 524320 | tf_op jit(solution)/shard_map/ppermute | solution.py:35
  324.1 5.9 %collective-permute-start.13 = (bf16[128,2048]{1,0:T(8,128)(2,1)}, bf16[128,2048]{1,0:T(8,128)(2,1)}, u32[]{:S(2)}, u32[]{:S(2)}) collective-permute-start(bf16[128,2048]{1,0:T(8,128)(2,1)} %collective-permute-done.12), channel_id=1, source_target_pairs={{1,0},{2,1},{3,2},{4,3},{5,4},{6,5},{7,6},{8,7},{9,8},{10,9},{11,1... | collective-permute-start | bytes 1572872 | tf_op jit(solution)/shard_map/ppermute | solution.py:37
  330.0 7.3 %collective-permute-done.6 = bf16[128,2048]{1,0:T(8,128)(2,1)} collective-permute-done((bf16[128,2048]{1,0:T(8,128)(2,1)S(1)}, bf16[128,2048]{1,0:T(8,128)(2,1)}, u32[]{:S(2)}, u32[]{:S(2)}) %collective-permute-start.6) | collective-permute-done | bytes 524320 | tf_op jit(solution)/shard_map/ppermute | solution.py:35
  339.1 12.8 %all-reduce.1 = bf16[512]{0:T(512)(128)(2,1)S(1)} all-reduce(bf16[512]{0:T(512)(128)(2,1)S(1)} %dynamic-update-slice), channel_id=1, replica_groups=mesh['grp'=8,'dev'=16] {'grp'}, use_global_device_ids=true, to_apply=%add.1 | all-reduce | flops 512 | bytes 2048
  377.9 8.4 %gather_fusion = bf16[16,128,2048]{2,1,0:T(8,128)(2,1)} fusion(bf16[16,128,2048]{2,1,0:T(8,128)(2,1)} %bitcast_dynamic-update-slice_fusion, s32[1024]{0:T(1024)S(1)} %pad_clamp_fusion), kind=kCustom, calls=%fused_computation | custom fusion | bytes 16777280 | tf_op jit(solution)/shard_map/gather | solution.py:41
  386.3 15.3 %convolution_convert_fusion = bf16[2048,2048]{1,0:T(8,128)(2,1)} fusion(bf16[512,2048]{1,0:T(8,128)(2,1)} %all-gather.5.cloned.1.call-done, bf16[2048,2048]{1,0:T(8,128)(2,1)} %bitcast.405, bf16[2048,512]{0,1:T(8,128)(2,1)} %all-gather.3.cloned.1.call-done, f32[512]{0:T(512)S(1)} %convert_element_type.97), kind=kOutput, calls=%fused_computation.18 | convolution fusion | flops 8604614656 | bytes 20973568 | tf_op jit(solution)/shard_map/dot_general | solution.py:244
  401.6 78.8 %reduce-scatter.2.cloned.1.call-done = bf16[128,2048]{1,0:T(8,128)(2,1)} async-done(((bf16[2048,2048]{1,0:T(8,128)(2,1)}), bf16[128,2048]{1,0:T(8,128)(2,1)}) %reduce-scatter.2.cloned.1.call-update) | async-done | bytes 524304 | tf_op jit(solution)/shard_map/reduce_scatter | solution.py:243
  (275 shorter events, 168.7 us)
Async XLA Ops:
  6.5 166.3 %copy-start = (bf16[128,2048]{1,0:T(8,128)(2,1)S(1)}, bf16[128,2048]{1,0:T(8,128)(2,1)}, u32[]{:S(2)}) copy-start(bf16[128,2048]{1,0:T(8,128)(2,1)} %param.19) | copy-start | bytes 1572868
  56.2 30.3 %all-to-all-start = ((bf16[128,32,128]{2,1,0:T(8,128)(2,1)}), bf16[128,32,128]{2,1,0:T(8,128)(2,1)S(1)}, u32[]{:S(2)}, u32[]{:S(2)}) async-start(bf16[128,32,128]{2,1,0:T(8,128)(2,1)} %bitcast.51), calls=%async_computation | async-start | bytes 2097152 | tf_op jit(solution)/shard_map/all_to_all | solution.py:185
  138.9 14.0 %all-to-all-start.1 = ((bf16[128,32,1]{1,2,0:T(2,128)(2,1)}), bf16[128,32,1]{1,2,0:T(2,128)(2,1)S(1)}, u32[]{:S(2)}, u32[]{:S(2)}) async-start(bf16[128,32,1]{1,2,0:T(2,128)(2,1)} %reshape.461), calls=%async_computation.1 | async-start | bytes 131072 | tf_op jit(solution)/shard_map/all_to_all | solution.py:196
  152.9 14.1 %all-to-all-start.2 = ((bf16[128,32,1]{1,2,0:T(2,128)(2,1)}), bf16[128,32,1]{1,2,0:T(2,128)(2,1)S(1)}, u32[]{:S(2)}, u32[]{:S(2)}) async-start(bf16[128,32,1]{1,2,0:T(2,128)(2,1)} %reshape.462), calls=%async_computation.2 | async-start | bytes 131072 | tf_op jit(solution)/shard_map/all_to_all | solution.py:197
  167.0 23.7 %all-to-all-start.3 = ((bf16[128,32,128]{2,1,0:T(8,128)(2,1)}), bf16[128,32,128]{2,1,0:T(8,128)(2,1)S(1)}, u32[]{:S(2)}, u32[]{:S(2)}) async-start(bf16[128,32,128]{2,1,0:T(8,128)(2,1)} %bitcast.107), calls=%async_computation.3 | async-start | bytes 2097152 | tf_op jit(solution)/shard_map/all_to_all | solution.py:195
  171.6 214.7 %all-gather.3.cloned.1.call-start = ((), (), s32[]{:S(2)}) async-start(), calls=%async_computation.5 | async-start | bytes 2359296 | tf_op jit(solution)/shard_map/all_gather | solution.py:238
  226.4 112.5 %copy-start.20 = (bf16[64]{0:T(256)(128)(2,1)S(1)}, bf16[64]{0:T(256)(128)(2,1)}, u32[]{:S(2)}) copy-start(bf16[64]{0:T(256)(128)(2,1)} %param.27) | copy-start | bytes 388
  237.8 16.2 %collective-permute-start = (bf16[128,2048]{1,0:T(8,128)(2,1)S(1)}, bf16[128,2048]{1,0:T(8,128)(2,1)S(1)}, u32[]{:S(2)}, u32[]{:S(2)}) collective-permute-start(bf16[128,2048]{1,0:T(8,128)(2,1)S(1)} %add_convert_fusion.1), channel_id=1, source_target_pairs={{0,1},{1,2},{2,3},{3,4},{4,5},{5,6},{6,7},{7,8},{8,9},{9,10},{10,1... | collective-permute-start | bytes 1572872 | tf_op jit(solution)/shard_map/ppermute | solution.py:35
  238.8 147.4 %all-gather.5.cloned.1.call-start = ((), (), s32[]{:S(2)}) async-start(), calls=%async_computation.6 | async-start | bytes 2359296 | tf_op jit(solution)/shard_map/all_gather | solution.py:240
  254.1 15.2 %collective-permute-start.1 = (bf16[128,2048]{1,0:T(8,128)(2,1)S(1)}, bf16[128,2048]{1,0:T(8,128)(2,1)S(1)}, u32[]{:S(2)}, u32[]{:S(2)}) collective-permute-start(bf16[128,2048]{1,0:T(8,128)(2,1)S(1)} %collective-permute-done), channel_id=1, source_target_pairs={{0,1},{1,2},{2,3},{3,4},{4,5},{5,6},{6,7},{7,8},{8,9},{9,10},{10,1... | collective-permute-start | bytes 1572872 | tf_op jit(solution)/shard_map/ppermute | solution.py:35
  254.1 15.2 %collective-permute-start.8 = (bf16[128,2048]{1,0:T(8,128)(2,1)S(1)}, bf16[128,2048]{1,0:T(8,128)(2,1)S(1)}, u32[]{:S(2)}, u32[]{:S(2)}) collective-permute-start(bf16[128,2048]{1,0:T(8,128)(2,1)S(1)} %add_convert_fusion.1), channel_id=1, source_target_pairs={{1,0},{2,1},{3,2},{4,3},{5,4},{6,5},{7,6},{8,7},{9,8},{10,9},{11,1... | collective-permute-start | bytes 1572872 | tf_op jit(solution)/shard_map/ppermute | solution.py:37
  269.3 14.3 %collective-permute-start.2 = (bf16[128,2048]{1,0:T(8,128)(2,1)S(1)}, bf16[128,2048]{1,0:T(8,128)(2,1)S(1)}, u32[]{:S(2)}, u32[]{:S(2)}) collective-permute-start(bf16[128,2048]{1,0:T(8,128)(2,1)S(1)} %collective-permute-done.1), channel_id=1, source_target_pairs={{0,1},{1,2},{2,3},{3,4},{4,5},{5,6},{6,7},{7,8},{8,9},{9,10},{10,1... | collective-permute-start | bytes 1572872 | tf_op jit(solution)/shard_map/ppermute | solution.py:35
  269.3 14.3 %collective-permute-start.9 = (bf16[128,2048]{1,0:T(8,128)(2,1)S(1)}, bf16[128,2048]{1,0:T(8,128)(2,1)S(1)}, u32[]{:S(2)}, u32[]{:S(2)}) collective-permute-start(bf16[128,2048]{1,0:T(8,128)(2,1)S(1)} %collective-permute-done.8), channel_id=1, source_target_pairs={{1,0},{2,1},{3,2},{4,3},{5,4},{6,5},{7,6},{8,7},{9,8},{10,9},{11,1... | collective-permute-start | bytes 1572872 | tf_op jit(solution)/shard_map/ppermute | solution.py:37
  283.6 13.4 %collective-permute-start.3 = (bf16[128,2048]{1,0:T(8,128)(2,1)S(1)}, bf16[128,2048]{1,0:T(8,128)(2,1)S(1)}, u32[]{:S(2)}, u32[]{:S(2)}) collective-permute-start(bf16[128,2048]{1,0:T(8,128)(2,1)S(1)} %collective-permute-done.2), channel_id=1, source_target_pairs={{0,1},{1,2},{2,3},{3,4},{4,5},{5,6},{6,7},{7,8},{8,9},{9,10},{10,1... | collective-permute-start | bytes 1572872 | tf_op jit(solution)/shard_map/ppermute | solution.py:35
  283.6 13.4 %collective-permute-start.10 = (bf16[128,2048]{1,0:T(8,128)(2,1)S(1)}, bf16[128,2048]{1,0:T(8,128)(2,1)S(1)}, u32[]{:S(2)}, u32[]{:S(2)}) collective-permute-start(bf16[128,2048]{1,0:T(8,128)(2,1)S(1)} %collective-permute-done.9), channel_id=1, source_target_pairs={{1,0},{2,1},{3,2},{4,3},{5,4},{6,5},{7,6},{8,7},{9,8},{10,9},{11,1... | collective-permute-start | bytes 1572872 | tf_op jit(solution)/shard_map/ppermute | solution.py:37
  297.0 12.5 %collective-permute-start.4 = (bf16[128,2048]{1,0:T(8,128)(2,1)S(1)}, bf16[128,2048]{1,0:T(8,128)(2,1)S(1)}, u32[]{:S(2)}, u32[]{:S(2)}) collective-permute-start(bf16[128,2048]{1,0:T(8,128)(2,1)S(1)} %collective-permute-done.3), channel_id=1, source_target_pairs={{0,1},{1,2},{2,3},{3,4},{4,5},{5,6},{6,7},{7,8},{8,9},{9,10},{10,1... | collective-permute-start | bytes 1572872 | tf_op jit(solution)/shard_map/ppermute | solution.py:35
  297.9 12.0 %collective-permute-start.11 = (bf16[128,2048]{1,0:T(8,128)(2,1)S(1)}, bf16[128,2048]{1,0:T(8,128)(2,1)S(1)}, u32[]{:S(2)}, u32[]{:S(2)}) collective-permute-start(bf16[128,2048]{1,0:T(8,128)(2,1)S(1)} %collective-permute-done.10), channel_id=1, source_target_pairs={{1,0},{2,1},{3,2},{4,3},{5,4},{6,5},{7,6},{8,7},{9,8},{10,9},{11,1... | collective-permute-start | bytes 1572872 | tf_op jit(solution)/shard_map/ppermute | solution.py:37
  309.5 13.5 %collective-permute-start.5 = (bf16[128,2048]{1,0:T(8,128)(2,1)S(1)}, bf16[128,2048]{1,0:T(8,128)(2,1)S(1)}, u32[]{:S(2)}, u32[]{:S(2)}) collective-permute-start(bf16[128,2048]{1,0:T(8,128)(2,1)S(1)} %collective-permute-done.4), channel_id=1, source_target_pairs={{0,1},{1,2},{2,3},{3,4},{4,5},{5,6},{6,7},{7,8},{8,9},{9,10},{10,1... | collective-permute-start | bytes 1572872 | tf_op jit(solution)/shard_map/ppermute | solution.py:35
  310.7 13.5 %collective-permute-start.12 = (bf16[128,2048]{1,0:T(8,128)(2,1)S(1)}, bf16[128,2048]{1,0:T(8,128)(2,1)}, u32[]{:S(2)}, u32[]{:S(2)}) collective-permute-start(bf16[128,2048]{1,0:T(8,128)(2,1)S(1)} %collective-permute-done.11), channel_id=1, source_target_pairs={{1,0},{2,1},{3,2},{4,3},{5,4},{6,5},{7,6},{8,7},{9,8},{10,9},{11,1... | collective-permute-start | bytes 1572872 | tf_op jit(solution)/shard_map/ppermute | solution.py:37
  323.0 14.4 %collective-permute-start.6 = (bf16[128,2048]{1,0:T(8,128)(2,1)S(1)}, bf16[128,2048]{1,0:T(8,128)(2,1)}, u32[]{:S(2)}, u32[]{:S(2)}) collective-permute-start(bf16[128,2048]{1,0:T(8,128)(2,1)S(1)} %collective-permute-done.5), channel_id=1, source_target_pairs={{0,1},{1,2},{2,3},{3,4},{4,5},{5,6},{6,7},{7,8},{8,9},{9,10},{10,1... | collective-permute-start | bytes 1572872 | tf_op jit(solution)/shard_map/ppermute | solution.py:35
  324.1 27.8 %collective-permute-start.13 = (bf16[128,2048]{1,0:T(8,128)(2,1)}, bf16[128,2048]{1,0:T(8,128)(2,1)}, u32[]{:S(2)}, u32[]{:S(2)}) collective-permute-start(bf16[128,2048]{1,0:T(8,128)(2,1)} %collective-permute-done.12), channel_id=1, source_target_pairs={{1,0},{2,1},{3,2},{4,3},{5,4},{6,5},{7,6},{8,7},{9,8},{10,9},{11,1... | collective-permute-start | bytes 1572872 | tf_op jit(solution)/shard_map/ppermute | solution.py:37
  337.4 19.6 %collective-permute-start.7 = (bf16[128,2048]{1,0:T(8,128)(2,1)}, bf16[128,2048]{1,0:T(8,128)(2,1)}, u32[]{:S(2)}, u32[]{:S(2)}) collective-permute-start(bf16[128,2048]{1,0:T(8,128)(2,1)} %collective-permute-done.6), channel_id=1, source_target_pairs={{0,1},{1,2},{2,3},{3,4},{4,5},{5,6},{6,7},{7,8},{8,9},{9,10},{10,1... | collective-permute-start | bytes 1572872 | tf_op jit(solution)/shard_map/ppermute | solution.py:35
  337.4 143.0 %reduce-scatter.2.cloned.1.call-start = ((), (), s32[]{:S(2)}) async-start(), calls=%async_computation.7 | async-start | bytes 8912896 | tf_op jit(solution)/shard_map/reduce_scatter | solution.py:243
  352.0 25.1 %collective-permute-start.14 = (bf16[128,2048]{1,0:T(8,128)(2,1)}, bf16[128,2048]{1,0:T(8,128)(2,1)S(1)}, u32[]{:S(2)}, u32[]{:S(2)}) collective-permute-start(bf16[128,2048]{1,0:T(8,128)(2,1)} %collective-permute-done.13), channel_id=1, source_target_pairs={{1,0},{2,1},{3,2},{4,3},{5,4},{6,5},{7,6},{8,7},{9,8},{10,9},{11,1... | collective-permute-start | bytes 1572872 | tf_op jit(solution)/shard_map/ppermute | solution.py:37
  (27 other events, 913.8 us)
Sparse Core Ops, SparseCore 0:
  239.0 23.3 all-gather.2
  337.5 25.2 all-gather.4
  401.7 78.6 reduce-scatter.1
